TPU v7x, 512 devices: a whole 4x8x8 slice. The times are simulated.
512 devices in a mesh: ep: 64 (over z, y), tp: 8 (over x, core).
Axes of the slice: x: 4, y: 8, z: 8, core: 2. Of those that a mesh axis runs over, the one named last changes fastest.
Arguments:
- patches: bfloat16 [32768, 1024], P('ep', 'tp'), may hold values from -6 to 6
- patch_grad: bfloat16 [32768, 1024], P('ep', 'tp'), may hold values from -1.796875 to 1.796875
- expert_up: bfloat16 [64, 1024, 4096], P('ep', None, 'tp'), may hold values from -0.1875 to 0.1875
- expert_down: bfloat16 [64, 4096, 1024], P('ep', 'tp'), may hold values from -0.09375 to 0.09375
- expert_counts: int32 [64, 64], P('ep'), may hold values from 1 to 16, as said below
Outputs:
- input_grad: bfloat16 [32768, 1024], P('ep', 'tp')
- up_grad: bfloat16 [64, 1024, 4096], P('ep', None, 'tp')
- down_grad: bfloat16 [64, 4096, 1024], P('ep', 'tp')
Inputs may be any that keep to these rules, and one draw needn't show every extreme that they name: `expert_counts`: row s gives, for each of the 64 experts in order, how many of the 512 rows of ep index s are routed to it; those rows stand together in expert order. Every row sums to 512, and one expert has exactly 16 rows from every index of ep.
All inputs are finite; a program needn't handle non-finite values.
Results may differ from a plain program's by a relative error of at most 0.0049.
Values may be sent and summed in bfloat16 or wider, within the bound.
No kernel may reach another device: no remote copies, remote signals or barrier semaphores. Data moves between devices by JAX's collectives and lax.ppermute only.
A program may use at most 64 MiB of HBM per device.

v0:
```python
import jax
import jax.numpy as jnp
from jax import lax
from jax.sharding import PartitionSpec as P


def activation(values):
    return jax.nn.gelu(values, approximate=True)


def slot_plan(counts_row, row_count, capacity):
    experts = counts_row.shape[0]
    row_ends = jnp.cumsum(counts_row)
    row_starts = row_ends - counts_row
    positions = lax.broadcasted_iota(jnp.int32, (experts, capacity), 1)
    slot_live = positions < counts_row[:, None]
    slot_source = jnp.where(slot_live, row_starts[:, None] + positions, 0)
    row_ids = lax.broadcasted_iota(jnp.int32, (row_count, experts), 0)
    row_expert = jnp.sum((row_ids >= row_ends[None, :]).astype(jnp.int32), axis=1)
    expert_ids = lax.broadcasted_iota(jnp.int32, (row_count, experts), 1)
    own_start = jnp.sum(
        jnp.where(row_expert[:, None] == expert_ids, row_starts[None, :], 0), axis=1
    )
    row_numbers = lax.broadcasted_iota(jnp.int32, (row_count,), 0)
    row_slot = row_expert * capacity + row_numbers - own_start
    return (slot_live, slot_source, row_slot)


def fill_slots(source_table, slot_live, slot_source):
    picked = jnp.take(source_table, slot_source.reshape(-1), axis=0)
    picked = picked.reshape(slot_source.shape + (source_table.shape[1],))
    return jnp.where(slot_live[:, :, None], picked, jnp.zeros((), source_table.dtype))


def per_device(patches, patch_grad, expert_up, expert_down, expert_counts):
    row_count = patches.shape[0]
    experts = expert_counts.shape[1]
    capacity = 2 * row_count // experts
    slot_live, slot_source, row_slot = slot_plan(expert_counts[0], row_count, capacity)
    weight_up = expert_up[0]
    weight_down = expert_down[0]
    gathered_rows, gathered_grads = (
        lax.all_gather(patches, "tp", axis=1, tiled=True),
        lax.all_gather(patch_grad, "tp", axis=1, tiled=True),
    )
    send_rows = fill_slots(gathered_rows, slot_live, slot_source)
    send_grads = fill_slots(gathered_grads, slot_live, slot_source)
    got_rows, got_grads = (
        lax.all_to_all(send_rows, "ep", split_axis=0, concat_axis=0, tiled=True),
        lax.all_to_all(send_grads, "ep", split_axis=0, concat_axis=0, tiled=True),
    )
    sources = got_rows.shape[0]
    feature_width = got_rows.shape[2]
    slot_rows = got_rows.reshape(sources * capacity, feature_width)
    slot_grads = got_grads.reshape(sources * capacity, feature_width)
    pre_act = jnp.dot(slot_rows, weight_up, preferred_element_type=jnp.float32)
    act_value, act_back = jax.vjp(activation, pre_act)
    hidden = act_value.astype(jnp.bfloat16)
    hidden_grad = lax.dot_general(
        slot_grads, weight_down, (((1,), (1,)), ((), ())), preferred_element_type=jnp.float32
    )
    pre_grad = act_back(hidden_grad)[0].astype(jnp.bfloat16)
    down_part = lax.dot_general(
        hidden, slot_grads, (((0,), (0,)), ((), ())), preferred_element_type=jnp.float32
    )
    up_part = lax.dot_general(
        slot_rows, pre_grad, (((0,), (0,)), ((), ())), preferred_element_type=jnp.float32
    )
    row_term = lax.dot_general(
        pre_grad, weight_up, (((1,), (1,)), ((), ())), preferred_element_type=jnp.float32
    )
    summed = lax.psum_scatter(row_term, "tp", scatter_dimension=1, tiled=True)
    back_rows = summed.astype(jnp.bfloat16).reshape(sources, capacity, summed.shape[1])
    returned = lax.all_to_all(back_rows, "ep", split_axis=0, concat_axis=0, tiled=True)
    input_grad = jnp.take(returned.reshape(experts * capacity, returned.shape[2]), row_slot, axis=0)
    return (input_grad, up_part.astype(jnp.bfloat16)[None], down_part.astype(jnp.bfloat16)[None])


def solution(mesh):
    return jax.shard_map(
        per_device,
        mesh=mesh,
        in_specs=(
            P("ep", "tp"),
            P("ep", "tp"),
            P("ep", None, "tp"),
            P("ep", "tp", None),
            P("ep", None),
        ),
        out_specs=(P("ep", "tp"), P("ep", None, "tp"), P("ep", "tp", None)),
        check_vma=False,
    )
```

profile of v0, /device:TPU:8, one launch (start us, length us, event | category | flops | bytes accessed | tf_op | source)
XLA Modules:
  0.0 298.1 jit_solution(2394442050553680179)
XLA Ops:
  7.2 0.7 all-gather.3.cloned.1.call-update
  8.0 0.7 all-gather.5.cloned.1.call-update
  8.7 0.7 copy.10
  9.4 0.1 reduce-window.4
  9.5 0.1 reduce
  9.6 0.7 bitcast_subtract_fusion.1
  10.3 0.7 add_select_fusion
  11.1 0.7 iota_compare_fusion.2
  11.9 31.4 %all-gather.3.cloned.1.call-done = bf16[512,1024]{1,0:T(8,128)(2,1)} async-done(((bf16[512,128]{1,0:T(8,128)(2,1)}), bf16[512,1024]{1,0:T(8,128)(2,1)}) %all-gather.3.cloned.1.call-update) | async-done | bytes 1048592 | tf_op jit(solution)/shard_map/all_gather | solution.py:44
  43.3 6.3 %gather_fusion.1 = bf16[1024,1024]{1,0:T(8,128)(2,1)S(1)} fusion(bf16[512,1024]{1,0:T(8,128)(2,1)} %all-gather.3.cloned.1.call-done, s32[1024]{0:T(1024)S(1)} %fusion.21), kind=kCustom, calls=%fused_computation.clone | custom fusion | bytes 4198400 | tf_op jit(solution)/shard_map/jit(_take)/gather | solution.py:30
  49.6 25.4 %all-gather.5.cloned.1.call-done = bf16[512,1024]{1,0:T(8,128)(2,1)} async-done(((bf16[512,128]{1,0:T(8,128)(2,1)}), bf16[512,1024]{1,0:T(8,128)(2,1)}) %all-gather.5.cloned.1.call-update) | async-done | bytes 1048592 | tf_op jit(solution)/shard_map/all_gather | solution.py:43
  75.0 7.4 %gather_fusion.2 = bf16[1024,1024]{1,0:T(8,128)(2,1)} fusion(bf16[512,1024]{1,0:T(8,128)(2,1)} %all-gather.5.cloned.1.call-done, s32[1024]{0:T(1024)S(1)} %fusion.21), kind=kCustom, calls=%fused_computation.1.clone | custom fusion | bytes 4198400 | tf_op jit(solution)/shard_map/jit(_take)/gather | solution.py:30
  82.4 2.0 broadcast_select_fusion.1
  84.5 1.7 broadcast_select_fusion.3
  86.2 66.0 %all_to_all.15 = bf16[64,16,1024]{2,1,0:T(8,128)(2,1)S(1)} all-to-all(bf16[64,16,1024]{2,1,0:T(8,128)(2,1)S(1)} %get-tuple-element.5), channel_id=1, replica_groups=mesh['ep'=64,'tp'=8] {'ep'}, dimensions={0} | all-to-all | bytes 4194304 | tf_op jit(solution)/shard_map/all_to_all | solution.py:49
  152.2 8.6 %all-to-all-start = ((bf16[64,16,1024]{2,1,0:T(8,128)(2,1)}), bf16[64,16,1024]{2,1,0:T(8,128)(2,1)}, u32[]{:S(2)}, u32[]{:S(2)}) async-start(bf16[64,16,1024]{2,1,0:T(8,128)(2,1)} %get-tuple-element.4), calls=%async_computation | async-start | bytes 4194304 | tf_op jit(solution)/shard_map/all_to_all | solution.py:50
  160.8 2.6 fusion.11
  163.4 49.6 %all-to-all-done = bf16[64,16,1024]{2,1,0:T(8,128)(2,1)} async-done(((bf16[64,16,1024]{2,1,0:T(8,128)(2,1)}), bf16[64,16,1024]{2,1,0:T(8,128)(2,1)}, u32[]{:S(2)}, u32[]{:S(2)}) %all-to-all-start) | async-done | bytes 2097184 | tf_op jit(solution)/shard_map/all_to_all | solution.py:50
  213.0 4.9 %fusion.6 = bf16[1024,512]{1,0:T(8,128)(2,1)S(1)} fusion(f32[1024,512]{1,0:T(8,128)} %fusion.11, bf16[1024,1024]{1,0:T(8,128)(2,1)} %bitcast.4, bf16[1,512,1024]{2,1,0:T(8,128)(2,1)} %param.10), kind=kOutput, calls=%fused_computation.11 | convolution fusion | flops 1084227584 | bytes 6291456 | tf_op jit(solution)/shard_map/dot_general | solution.py:59
  217.9 1.0 copy-done.2
  218.9 3.2 %fusion.9 = f32[1024,1024]{1,0:T(8,128)} fusion(bf16[1024,512]{1,0:T(8,128)(2,1)S(1)} %fusion.6, bf16[1,1024,512]{2,1,0:T(8,128)(2,1)S(1)} %copy-done), kind=kOutput, calls=%fused_computation.21 | convolution fusion | flops 1073741824 | bytes 6291456 | tf_op jit(solution)/shard_map/dot_general | solution.py:69
  222.1 0.1 convert_reduce_fusion
  222.2 0.5 copy-done.1
  222.8 0.1 select_reduce_fusion
  222.9 38.3 %reduce-scatter.2.cloned.1.call-done = f32[1024,128]{1,0:T(8,128)} async-done(((f32[1024,1024]{1,0:T(8,128)}), f32[1024,128]{1,0:T(8,128)}) %reduce-scatter.2.cloned.1.call-update) | async-done | bytes 524304 | tf_op jit(solution)/shard_map/reduce_scatter | solution.py:72
  261.2 1.8 convert_element_type.20
  263.0 13.4 %all-to-all-start.2 = ((bf16[64,16,128]{2,1,0:T(8,128)(2,1)}), bf16[64,16,128]{2,1,0:T(8,128)(2,1)S(1)}, u32[]{:S(2)}, u32[]{:S(2)}) async-start(bf16[64,16,128]{2,1,0:T(8,128)(2,1)} %bitcast.43), calls=%async_computation.3 | async-start | bytes 524288 | tf_op jit(solution)/shard_map/all_to_all | solution.py:74
  276.4 3.6 %fusion.7 = bf16[1,1024,512]{2,1,0:T(8,128)(2,1)} fusion(bf16[1024,1024]{1,0:T(8,128)(2,1)S(1)} %bitcast.42, bf16[1024,512]{1,0:T(8,128)(2,1)} %copy-done.2), kind=kOutput, calls=%fused_computation.19 | convolution fusion | flops 1074266112 | bytes 4194304 | tf_op jit(solution)/shard_map/dot_general | solution.py:66
  280.0 4.0 %fusion.8 = bf16[1,512,1024]{2,1,0:T(8,128)(2,1)} fusion(bf16[1024,1024]{1,0:T(8,128)(2,1)} %bitcast.4, f32[1024,512]{1,0:T(8,128)S(1)} %copy-done.3), kind=kOutput, calls=%fused_computation.20 | convolution fusion | flops 1078984704 | bytes 5242880 | tf_op jit(solution)/shard_map/dot_general | solution.py:63
  284.0 5.4 %all-to-all-done.2 = bf16[64,16,128]{2,1,0:T(8,128)(2,1)S(1)} async-done(((bf16[64,16,128]{2,1,0:T(8,128)(2,1)}), bf16[64,16,128]{2,1,0:T(8,128)(2,1)S(1)}, u32[]{:S(2)}, u32[]{:S(2)}) %all-to-all-start.2) | async-done | bytes 262176 | tf_op jit(solution)/shard_map/all_to_all | solution.py:74
  289.4 1.3 gather_fusion
  290.8 0.8 broadcast_select_fusion.4
  (18 shorter events, 0.3 us)
Async XLA Ops:
  7.2 153.7 %copy-start = (bf16[1,1024,512]{2,1,0:T(8,128)(2,1)S(1)}, bf16[1,1024,512]{2,1,0:T(8,128)(2,1)}, u32[]{:S(2)}) copy-start(bf16[1,1024,512]{2,1,0:T(8,128)(2,1)} %param.9) | copy-start | bytes 3145732
  7.2 36.1 %all-gather.3.cloned.1.call-start = ((), (), s32[]{:S(2)}) async-start(), calls=%async_computation.4 | async-start | bytes 1179648 | tf_op jit(solution)/shard_map/all_gather | solution.py:44
  7.9 67.1 %all-gather.5.cloned.1.call-start = ((), (), s32[]{:S(2)}) async-start(), calls=%async_computation.5 | async-start | bytes 1179648 | tf_op jit(solution)/shard_map/all_gather | solution.py:43
  152.2 60.8 %all-to-all-start = ((bf16[64,16,1024]{2,1,0:T(8,128)(2,1)}), bf16[64,16,1024]{2,1,0:T(8,128)(2,1)}, u32[]{:S(2)}, u32[]{:S(2)}) async-start(bf16[64,16,1024]{2,1,0:T(8,128)(2,1)} %get-tuple-element.4), calls=%async_computation | async-start | bytes 4194304 | tf_op jit(solution)/shard_map/all_to_all | solution.py:50
  160.8 100.5 %reduce-scatter.2.cloned.1.call-start = ((), (), s32[]{:S(2)}) async-start(), calls=%async_computation.6 | async-start | bytes 4718592 | tf_op jit(solution)/shard_map/reduce_scatter | solution.py:72
  217.9 1.0 copy-start.2
  222.1 0.7 copy-start.1
  263.0 26.4 %all-to-all-start.2 = ((bf16[64,16,128]{2,1,0:T(8,128)(2,1)}), bf16[64,16,128]{2,1,0:T(8,128)(2,1)S(1)}, u32[]{:S(2)}, u32[]{:S(2)}) async-start(bf16[64,16,128]{2,1,0:T(8,128)(2,1)} %bitcast.43), calls=%async_computation.3 | async-start | bytes 524288 | tf_op jit(solution)/shard_map/all_to_all | solution.py:74
  276.4 3.6 %copy-start.3 = (f32[1024,512]{1,0:T(8,128)S(1)}, f32[1024,512]{1,0:T(8,128)}, u32[]{:S(2)}) copy-start(f32[1024,512]{1,0:T(8,128)} %fusion.11) | copy-start | bytes 6291460
Sparse Core Ops, SparseCore 0:
  10.1 33.1 all-gather.2
  45.4 29.5 all-gather.4
  222.3 38.9 reduce-scatter.1
where the time goes:
time: 299 us; the launch traced here: 298 us
  waiting for transfers between devices  152 us (51%)
  blocking collectives  66 us (22%)
  starting transfers between devices  22.1 us (7%)
  matrix products  18.3 us (6%)
  local copies, waits for them, and re-layouts  17.4 us (6%)
  between operations  13.9 us (5%)
  other arithmetic  8.85 us (3%)
    all_to_all x1, blocking collectives, per_device(): lax.all_to_all(send_rows, 'ep', split_axis=0, concat_axis=0, tiled=True)  66 us
    all_to_all x1, waiting for transfers between devices, per_device(): lax.all_to_all(send_grads, 'ep', split_axis=0, concat_axis=0, tiled=True)  49.6 us
    reduce_scatter x1, waiting for transfers between devices, per_device(): summed = lax.psum_scatter(row_term, 'tp', scatter_dimension=1, tiled=True)  38.3 us
    all_gather x1, waiting for transfers between devices, per_device(): lax.all_gather(patch_grad, 'tp', axis=1, tiled=True)  31.4 us
    all_gather x1, waiting for transfers between devices, per_device(): lax.all_gather(patches, 'tp', axis=1, tiled=True)  25.4 us
    gather x2, local copies, waits for them, and re-layouts, fill_slots(): picked = jnp.take(source_table, slot_source.reshape(-1), axis=0)  13.7 us
    all_to_all x1, starting transfers between devices, per_device(): lax.all_to_all(back_rows, 'ep', split_axis=0, concat_axis=0, tiled=True)  13.4 us
    all_to_all x1, starting transfers between devices, per_device(): lax.all_to_all(send_grads, 'ep', split_axis=0, concat_axis=0, tiled=True)  8.57 us
  transfers between devices with their start and end apart: 5, of which 5 were waited for; matrix products, arithmetic and copies ran while one was open for 7% of the time, Pallas kernels for 0%

commit v1 on v0

v1 whole, which is shorter than its diff:
```python
import jax
import jax.numpy as jnp
from jax import lax
from jax.experimental import pallas as pl
from jax.experimental.pallas import tpu as pltpu
from jax.sharding import Mesh, PartitionSpec as P

F32 = jnp.float32
BF16 = jnp.bfloat16
LANES = 128
ROW_STEPS = 4


def slot_onehot(counts, capacity, row_count):
    experts = counts.shape[1]
    slots = experts * capacity
    slot_ids = lax.broadcasted_iota(jnp.int32, (slots, experts), 0)
    expert_ids = lax.broadcasted_iota(jnp.int32, (slots, experts), 1)
    slot_expert = slot_ids // capacity
    zero = jnp.zeros((), jnp.int32)
    starts = jnp.sum(jnp.where(expert_ids < slot_expert, counts, zero), axis=1, keepdims=True)
    own = jnp.sum(jnp.where(expert_ids == slot_expert, counts, zero), axis=1, keepdims=True)
    position = lax.broadcasted_iota(jnp.int32, (slots, 1), 0) % capacity
    row_of_slot = jnp.where(position < own, starts + position, -1)
    rows = lax.broadcasted_iota(jnp.int32, (slots, row_count), 1)
    return jnp.where(rows == row_of_slot, 1.0, 0.0).astype(BF16)


def fill_kernel(counts_ref, rows_ref, grads_ref, out_ref):
    experts, _, capacity, width = out_ref.shape
    onehot = slot_onehot(counts_ref[...], capacity, rows_ref.shape[0])
    for which, ref in enumerate((rows_ref, grads_ref)):
        picked = jnp.dot(onehot, ref[...], preferred_element_type=F32)
        out_ref[:, which] = picked.astype(BF16).reshape(experts, capacity, width)


def fill_slots(counts, rows, grads, experts, capacity):
    return pl.pallas_call(
        fill_kernel,
        out_shape=jax.ShapeDtypeStruct((experts, 2, capacity, rows.shape[1]), BF16),
        name="fill_slots",
    )(counts, rows, grads)


def unfill_kernel(counts_ref, slots_ref, out_ref):
    experts, capacity, width = slots_ref.shape
    onehot = slot_onehot(counts_ref[...], capacity, out_ref.shape[0])
    table = slots_ref[...].reshape(experts * capacity, width)
    picked = lax.dot_general(onehot, table, (((0,), (0,)), ((), ())), preferred_element_type=F32)
    out_ref[...] = picked.astype(BF16)


def unfill_slots(counts, slots, row_count):
    return pl.pallas_call(
        unfill_kernel,
        out_shape=jax.ShapeDtypeStruct((row_count, slots.shape[2]), BF16),
        name="unfill_slots",
    )(counts, slots)


def expert_kernel(place_ref, own, left, right, far_lo, far_hi, own2, left2, right2, far_lo2, far_hi2,
                  up_ref, down_ref, x_ref, g_ref, hid_ref, pg_ref, theirs_ref, mine_ref, row_scr):
    step = pl.program_id(0)
    steps = pl.num_programs(0)
    at = place_ref[0]
    core = place_ref[1]
    rows = x_ref.shape[0]
    chips = theirs_ref.shape[0]

    def put(ref, shift, which):
        block = lax.rem(at + shift, chips) * 2 + which
        lanes = pl.ds(pl.multiple_of(block * LANES, LANES), LANES)
        x_ref[:, lanes] = ref[:, 0].reshape(rows, LANES)
        g_ref[:, lanes] = ref[:, 1].reshape(rows, LANES)

    for refs, which in (((own, left, right, far_lo, far_hi), core), ((own2, left2, right2, far_lo2, far_hi2), 1 - core)):
        put(refs[0], 0, which)
        put(refs[1], 3, which)
        put(refs[2], 1, which)

        @pl.when(step < steps // 2)
        def _():
            put(refs[3], 2, which)

        @pl.when(step >= steps // 2)
        def _():
            put(refs[4], 2, which)

    up = up_ref[...]
    pre = jnp.dot(x_ref[...], up, preferred_element_type=F32)
    hidden_grad = lax.dot_general(g_ref[...], down_ref[...], (((1,), (1,)), ((), ())), preferred_element_type=F32)
    scale = 0.7978845608028654
    square = pre * pre
    tanh = jnp.tanh(scale * (pre + 0.044715 * (square * pre)))
    half = 0.5 * (1.0 + tanh)
    hid_ref[...] = (pre * half).astype(BF16)
    slope = half + 0.5 * pre * (1.0 - tanh * tanh) * (scale * (1.0 + (3.0 * 0.044715) * square))
    pre_grad = (hidden_grad * slope).astype(BF16)
    pg_ref[...] = pre_grad
    row_scr[...] = lax.dot_general(pre_grad, up, (((1,), (1,)), ((), ())), preferred_element_type=F32)
    for chip in range(chips):
        own_lanes = pl.ds(pl.multiple_of((2 * chip + core) * LANES, LANES), LANES)
        their_lanes = pl.ds(pl.multiple_of((2 * chip + 1 - core) * LANES, LANES), LANES)
        mine_ref[chip] = row_scr[:, own_lanes]
        theirs_ref[chip] = row_scr[:, their_lanes].astype(BF16)


def expert_compute(place, pieces, pieces2, up, down):
    own = pieces[0]
    sources, _, capacity, _ = own.shape
    slots = sources * capacity
    width, hidden = up.shape
    part = sources // ROW_STEPS
    rows = part * capacity
    half_steps = ROW_STEPS // 2
    block = (part, 2, capacity, LANES)
    whole = pl.BlockSpec(block, lambda i: (i, 0, 0, 0))
    low = pl.BlockSpec(block, lambda i: (jnp.minimum(i, half_steps - 1), 0, 0, 0))
    high = pl.BlockSpec(block, lambda i: (jnp.maximum(i - half_steps, 0), 0, 0, 0))
    chunk_specs = [whole, whole, whole, low, high]
    row_block = lambda n: pl.BlockSpec((rows, n), lambda i: (i, 0))
    chip_block = pl.BlockSpec((width // (2 * LANES), rows, LANES), lambda i: (0, i, 0))
    chips = width // (2 * LANES)
    return pl.pallas_call(
        expert_kernel,
        grid=(ROW_STEPS,),
        in_specs=[pl.BlockSpec(memory_space=pltpu.SMEM)] + chunk_specs * 2 + [
            pl.BlockSpec(up.shape, lambda i: (0, 0)),
            pl.BlockSpec(down.shape, lambda i: (0, 0)),
        ],
        out_specs=[row_block(width), row_block(width), row_block(hidden), row_block(hidden), chip_block, chip_block],
        out_shape=[
            jax.ShapeDtypeStruct((slots, width), BF16),
            jax.ShapeDtypeStruct((slots, width), BF16),
            jax.ShapeDtypeStruct((slots, hidden), BF16),
            jax.ShapeDtypeStruct((slots, hidden), BF16),
            jax.ShapeDtypeStruct((chips, slots, LANES), BF16),
            jax.ShapeDtypeStruct((chips, slots, LANES), F32),
        ],
        scratch_shapes=[pltpu.VMEM((rows, width), F32)],
        name="expert_compute",
    )(place, *pieces, *pieces2, up, down)


def to_right(value):
    return lax.ppermute(value, "x", [(i, (i + 1) % 4) for i in range(4)])


def to_left(value):
    return lax.ppermute(value, "x", [(i, (i - 1) % 4) for i in range(4)])


def to_other_core(value):
    return lax.ppermute(value, "core", [(0, 1), (1, 0)])


def per_device(patches, patch_grad, expert_up, expert_down, expert_counts):
    row_count = patches.shape[0]
    experts = expert_counts.shape[1]
    capacity = 2 * row_count // experts
    up = expert_up[0]
    down = expert_down[0]
    place = jnp.stack([lax.axis_index("x"), lax.axis_index("core")]).astype(jnp.int32)
    send = fill_slots(expert_counts, patches, patch_grad, experts, capacity)
    own = lax.all_to_all(send, "ep", split_axis=0, concat_axis=0, tiled=True)
    left = to_right(own)
    right = to_left(own)
    half = own.shape[0] // 2
    far_lo = to_right(left[:half])
    far_hi = to_left(right[half:])
    pieces = (own, left, right, far_lo, far_hi)
    pieces2 = tuple(to_other_core(piece) for piece in pieces)
    slot_rows, slot_grads, hidden, pre_grad, theirs, mine = expert_compute(place, pieces, pieces2, up, down)
    chip_sum = (mine + to_other_core(theirs).astype(F32)).astype(BF16)
    parts = lax.all_to_all(chip_sum, "x", split_axis=0, concat_axis=0, tiled=True)
    wide = parts.astype(F32)
    summed = ((wide[0] + wide[1]) + (wide[2] + wide[3])).astype(BF16)
    back = summed.reshape(experts, capacity, summed.shape[1])
    returned = lax.all_to_all(back, "ep", split_axis=0, concat_axis=0, tiled=True)
    down_part = lax.dot_general(hidden, slot_grads, (((0,), (0,)), ((), ())), preferred_element_type=F32)
    up_part = lax.dot_general(slot_rows, pre_grad, (((0,), (0,)), ((), ())), preferred_element_type=F32)
    input_grad = unfill_slots(expert_counts, returned, row_count)
    return (input_grad, up_part.astype(BF16)[None], down_part.astype(BF16)[None])


def solution(mesh):
    fine = Mesh(mesh.devices.reshape(mesh.shape["ep"], mesh.shape["tp"] // 2, 2), ("ep", "x", "core"))
    tp = ("x", "core")
    return jax.shard_map(
        per_device,
        mesh=fine,
        in_specs=(P("ep", tp), P("ep", tp), P("ep", None, tp), P("ep", tp, None), P("ep", None)),
        out_specs=(P("ep", tp), P("ep", None, tp), P("ep", tp, None)),
        check_vma=False,
    )
```

time: 299 us -> 134 us (0.45)
  waiting for transfers between devices: 152 us -> 19.5 us
  local copies, waits for them, and re-layouts: 17.4 us -> 1.72 us
  Pallas kernels: 0 us -> 15.4 us
  matrix products: 18.3 us -> 4.49 us
  between operations: 13.9 us -> 0.88 us
  blocking collectives: 66 us -> 54.7 us
  starting transfers between devices: 22.1 us -> 33.3 us
  other arithmetic: 8.85 us -> 3.4 us
    all_gather x2 -> x0, waiting for transfers between devices: 56.8 us -> none  [the longest x1 31.4 us: per_device(): lax.all_gather(patch_grad, 'tp', axis=1, tiled=True)]
    all_to_all x2 -> x1, waiting for transfers between devices: 54.9 us -> 9.19 us  [per_device(): lax.all_to_all(back, 'ep', split_axis=0, concat_axis=0, tiled=True)]
    reduce_scatter x1 -> x0, waiting for transfers between devices: 38.3 us -> none  [per_device(): summed = lax.psum_scatter(row_term, 'tp', scatter_dimension=1, tiled=True)]
    ppermute x0 -> x10, starting transfers between devices: none -> 26.2 us  [the longest x6 12.1 us: to_other_core(): return lax.ppermute(value, 'core', [(0, 1), (1, 0)])]
    pallas_call x0 -> x3, Pallas kernels: none -> 15.4 us  [the longest x1 9.87 us: expert_compute(): pl.pallas_call(expert_kernel, grid=(ROW_STEPS,), in_specs=[pl.BlockSpec(m...]
    gather x3 -> x0, local copies, waits for them, and re-layouts: 15.1 us -> none  [the longest x2 13.7 us: fill_slots(): picked = jnp.take(source_table, slot_source.reshape(-1), axis=0)]
    all_to_all x2 -> x1, starting transfers between devices: 22 us -> 7.12 us  [per_device(): lax.all_to_all(back, 'ep', split_axis=0, concat_axis=0, tiled=True)]
    all_to_all x1 -> x2, blocking collectives: 66 us -> 54.7 us  [the longest x1 36 us: per_device(): own = lax.all_to_all(send, 'ep', split_axis=0, concat_axis=0, tiled=True)]
  transfers between devices with their start and end apart: 5 -> 11, of which waited for: 5 -> 5; matrix products, arithmetic and copies ran while one was open for 7% -> 4% of each run, Pallas kernels for 0% -> 0%
where the time goes in v1:
time: 134 us; the launch traced here: 133 us
  blocking collectives  54.7 us (41%)
  starting transfers between devices  33.3 us (25%)
  waiting for transfers between devices  19.5 us (15%)
  Pallas kernels  15.4 us (11%)
  matrix products  4.49 us (3%)
  other arithmetic  3.4 us (3%)
  local copies, waits for them, and re-layouts  1.72 us (1%)
    all_to_all x1, blocking collectives, per_device(): own = lax.all_to_all(send, 'ep', split_axis=0, concat_axis=0, tiled=True)  36 us
    all_to_all x1, blocking collectives, per_device(): lax.all_to_all(chip_sum, 'x', split_axis=0, concat_axis=0, tiled=True)  18.7 us
    ppermute x6, starting transfers between devices, to_other_core(): return lax.ppermute(value, 'core', [(0, 1), (1, 0)])  12.1 us
    ppermute x2, starting transfers between devices, to_left(): return lax.ppermute(value, 'x', [(i, (i - 1) % 4) for i in range(4)])  10.3 us
    pallas_call x1, Pallas kernels, expert_compute(): pl.pallas_call(expert_kernel, grid=(ROW_STEPS,), in_specs=[pl.BlockSpec(m...  9.87 us
    all_to_all x1, waiting for transfers between devices, per_device(): lax.all_to_all(back, 'ep', split_axis=0, concat_axis=0, tiled=True)  9.19 us
    all_to_all x1, starting transfers between devices, per_device(): lax.all_to_all(back, 'ep', split_axis=0, concat_axis=0, tiled=True)  7.12 us
    ppermute x2, waiting for transfers between devices, to_left(): return lax.ppermute(value, 'x', [(i, (i - 1) % 4) for i in range(4)])  5.04 us
  transfers between devices with their start and end apart: 11, of which 5 were waited for; matrix products, arithmetic and copies ran while one was open for 4% of the time, Pallas kernels for 0%

profile of v1, /device:TPU:8, one launch (start us, length us, event | category | flops | bytes accessed | tf_op | source)
XLA Modules:
  0.0 133.5 jit_solution(6448068984871770779)
XLA Ops:
  0.6 2.8 %fill_slots.1 = bf16[64,2,16,128]{3,2,1,0:T(8,128)(2,1)} custom-call(s32[1,64]{1,0:T(1,128)} %counts_ref.3, bf16[512,128]{1,0:T(8,128)(2,1)} %rows_ref.1, bf16[512,128]{1,0:T(8,128)(2,1)} %grads_ref.1), custom_call_target="tpu_custom_call" | custom-call | tf_op jit(solution)/shard_map/fill_slots/pallas_call | solution.py:38
  3.4 36.0 %all_to_all.15.own = bf16[64,2,16,128]{3,2,1,0:T(8,128)(2,1)S(1)} all-to-all(bf16[64,2,16,128]{3,2,1,0:T(8,128)(2,1)} %fill_slots.1), channel_id=1, replica_groups=mesh['ep'=64,'x'=4,'core'=2] {'ep'}, dimensions={0} | all-to-all | bytes 1048576 | tf_op jit(solution)/shard_map/all_to_all | solution.py:165
  39.4 4.7 %collective-permute-start.1 = (bf16[64,2,16,128]{3,2,1,0:T(8,128)(2,1)S(1)}, bf16[64,2,16,128]{3,2,1,0:T(8,128)(2,1)S(1)}, u32[]{:S(2)}, u32[]{:S(2)}) collective-permute-start(bf16[64,2,16,128]{3,2,1,0:T(8,128)(2,1)S(1)} %all_to_all.15.own), channel_id=1, source_target_pairs={{0,6},{2,0},{4,2},{6,4},{1,7},{3,1},{5,3},{7,5},{8,14},{10,8},{12,... | collective-permute-start | bytes 1572872 | tf_op jit(solution)/shard_map/ppermute | solution.py:150
  44.1 1.9 %collective-permute-start = (bf16[64,2,16,128]{3,2,1,0:T(8,128)(2,1)S(1)}, bf16[64,2,16,128]{3,2,1,0:T(8,128)(2,1)S(1)}, u32[]{:S(2)}, u32[]{:S(2)}) collective-permute-start(bf16[64,2,16,128]{3,2,1,0:T(8,128)(2,1)S(1)} %all_to_all.15.own), channel_id=1, source_target_pairs={{0,2},{2,4},{4,6},{6,0},{1,3},{3,5},{5,7},{7,1},{8,10},{10,12},{12... | collective-permute-start | bytes 1572872 | tf_op jit(solution)/shard_map/ppermute | solution.py:146
  46.0 1.9 %collective-permute-start.4 = (bf16[64,2,16,128]{3,2,1,0:T(8,128)(2,1)S(1)}, bf16[64,2,16,128]{3,2,1,0:T(8,128)(2,1)S(1)}, u32[]{:S(2)}, u32[]{:S(2)}) collective-permute-start(bf16[64,2,16,128]{3,2,1,0:T(8,128)(2,1)S(1)} %all_to_all.15.own), channel_id=1, source_target_pairs={{0,1},{1,0},{2,3},{3,2},{4,5},{5,4},{6,7},{7,6},{8,9},{9,8},{10,11... | collective-permute-start | bytes 1572872 | tf_op jit(solution)/shard_map/ppermute | solution.py:154
  47.9 5.0 %collective-permute-done.1.right = bf16[64,2,16,128]{3,2,1,0:T(8,128)(2,1)S(1)} collective-permute-done((bf16[64,2,16,128]{3,2,1,0:T(8,128)(2,1)S(1)}, bf16[64,2,16,128]{3,2,1,0:T(8,128)(2,1)S(1)}, u32[]{:S(2)}, u32[]{:S(2)}) %collective-permute-start.1) | collective-permute-done | bytes 524320 | tf_op jit(solution)/shard_map/ppermute | solution.py:150
  53.0 5.6 %collective-permute-start.3 = (bf16[32,2,16,128]{3,2,1,0:T(8,128)(2,1)S(1)}, bf16[32,2,16,128]{3,2,1,0:T(8,128)(2,1)S(1)}, u32[]{:S(2)}, u32[]{:S(2)}) collective-permute-start(bf16[32,2,16,128]{3,2,1,0:T(8,128)(2,1)S(1)} %slice.25), channel_id=1, source_target_pairs={{0,6},{2,0},{4,2},{6,4},{1,7},{3,1},{5,3},{7,5},{8,14},{10,8},{12,... | collective-permute-start | bytes 786440 | tf_op jit(solution)/shard_map/ppermute | solution.py:150
  58.6 0.0 collective-permute-done.left
  58.7 1.9 %collective-permute-start.2 = (bf16[32,2,16,128]{3,2,1,0:T(8,128)(2,1)S(1)}, bf16[32,2,16,128]{3,2,1,0:T(8,128)(2,1)}, u32[]{:S(2)}, u32[]{:S(2)}) collective-permute-start(bf16[32,2,16,128]{3,2,1,0:T(8,128)(2,1)S(1)} %slice.24), channel_id=1, source_target_pairs={{0,2},{2,4},{4,6},{6,0},{1,3},{3,5},{5,7},{7,1},{8,10},{10,12},{12... | collective-permute-start | bytes 786440 | tf_op jit(solution)/shard_map/ppermute | solution.py:146
  60.6 1.9 %collective-permute-start.6 = (bf16[64,2,16,128]{3,2,1,0:T(8,128)(2,1)S(1)}, bf16[64,2,16,128]{3,2,1,0:T(8,128)(2,1)S(1)}, u32[]{:S(2)}, u32[]{:S(2)}) collective-permute-start(bf16[64,2,16,128]{3,2,1,0:T(8,128)(2,1)S(1)} %collective-permute-done.1.right), channel_id=1, source_target_pairs={{0,1},{1,0},{2,3},{3,2},{4,5},{5,4},{6,7},{7,6},{8,9},{9,8},{10,11... | collective-permute-start | bytes 1572872 | tf_op jit(solution)/shard_map/ppermute | solution.py:154
  62.5 2.4 %collective-permute-start.5 = (bf16[64,2,16,128]{3,2,1,0:T(8,128)(2,1)S(1)}, bf16[64,2,16,128]{3,2,1,0:T(8,128)(2,1)S(1)}, u32[]{:S(2)}, u32[]{:S(2)}) collective-permute-start(bf16[64,2,16,128]{3,2,1,0:T(8,128)(2,1)S(1)} %collective-permute-done.left), channel_id=1, source_target_pairs={{0,1},{1,0},{2,3},{3,2},{4,5},{5,4},{6,7},{7,6},{8,9},{9,8},{10,11... | collective-permute-start | bytes 1572872 | tf_op jit(solution)/shard_map/ppermute | solution.py:154
  65.0 1.9 %collective-permute-start.8 = (bf16[32,2,16,128]{3,2,1,0:T(8,128)(2,1)S(1)}, bf16[32,2,16,128]{3,2,1,0:T(8,128)(2,1)}, u32[]{:S(2)}, u32[]{:S(2)}) collective-permute-start(bf16[32,2,16,128]{3,2,1,0:T(8,128)(2,1)S(1)} %collective-permute-done.3.far_hi), channel_id=1, source_target_pairs={{0,1},{1,0},{2,3},{3,2},{4,5},{5,4},{6,7},{7,6},{8,9},{9,8},{10,11... | collective-permute-start | bytes 786440 | tf_op jit(solution)/shard_map/ppermute | solution.py:154
  66.9 1.4 %collective-permute-done.2.far_lo = bf16[32,2,16,128]{3,2,1,0:T(8,128)(2,1)} collective-permute-done((bf16[32,2,16,128]{3,2,1,0:T(8,128)(2,1)S(1)}, bf16[32,2,16,128]{3,2,1,0:T(8,128)(2,1)}, u32[]{:S(2)}, u32[]{:S(2)}) %collective-permute-start.2) | collective-permute-done | bytes 262176 | tf_op jit(solution)/shard_map/ppermute | solution.py:146
  68.2 1.9 %collective-permute-start.7 = (bf16[32,2,16,128]{3,2,1,0:T(8,128)(2,1)}, bf16[32,2,16,128]{3,2,1,0:T(8,128)(2,1)}, u32[]{:S(2)}, u32[]{:S(2)}) collective-permute-start(bf16[32,2,16,128]{3,2,1,0:T(8,128)(2,1)} %collective-permute-done.2.far_lo), channel_id=1, source_target_pairs={{0,1},{1,0},{2,3},{3,2},{4,5},{5,4},{6,7},{7,6},{8,9},{9,8},{10,11... | collective-permute-start | bytes 786440 | tf_op jit(solution)/shard_map/ppermute | solution.py:154
  70.2 0.6 pad_add_fusion.place_ref
  70.8 1.2 collective-permute-done.7.far_lo2
  72.1 0.8 copy-done.7
  72.8 0.2 copy-done.8
  73.0 9.9 %expert_compute.1 = (bf16[1024,1024]{1,0:T(8,128)(2,1)}, bf16[1024,1024]{1,0:T(8,128)(2,1)}, bf16[1024,512]{1,0:T(8,128)(2,1)}, bf16[1024,512]{1,0:T(8,128)(2,1)...) custom-call(s32[2]{0:T(128)} %pad_add_fusion.place_ref, bf16[64,2,16,128]{3,2,1,0:T(8,128)(2,1)} %copy-done, ...), custom_call_target="tpu_custom_call" | custom-call | tf_op jit(solution)/shard_map/expert_compute/pallas_call | solution.py:124
  82.9 2.0 %collective-permute-start.9 = (bf16[4,1024,128]{2,1,0:T(8,128)(2,1)}, bf16[4,1024,128]{2,1,0:T(8,128)(2,1)S(1)}, u32[]{:S(2)}, u32[]{:S(2)}) collective-permute-start(bf16[4,1024,128]{2,1,0:T(8,128)(2,1)} %get-tuple-element.10), channel_id=1, source_target_pairs={{0,1},{1,0},{2,3},{3,2},{4,5},{5,4},{6,7},{7,6},{8,9},{9,8},{10,11... | collective-permute-start | bytes 3145736 | tf_op jit(solution)/shard_map/ppermute | solution.py:154
  84.9 2.7 %collective-permute-done.9 = bf16[4,1024,128]{2,1,0:T(8,128)(2,1)S(1)} collective-permute-done((bf16[4,1024,128]{2,1,0:T(8,128)(2,1)}, bf16[4,1024,128]{2,1,0:T(8,128)(2,1)S(1)}, u32[]{:S(2)}, u32[]{:S(2)}) %collective-permute-start.9) | collective-permute-done | bytes 1048608 | tf_op jit(solution)/shard_map/ppermute | solution.py:154
  87.6 1.8 %add_convert_fusion = bf16[4,1024,128]{2,1,0:T(8,128)(2,1)S(1)} fusion(f32[4,1024,128]{2,1,0:T(8,128)} %get-tuple-element.9, bf16[4,1024,128]{2,1,0:T(8,128)(2,1)S(1)} %collective-permute-done.9), kind=kLoop, calls=%fused_computation | loop fusion | flops 1572864 | bytes 4194304 | tf_op jit(solution)/shard_map/convert_element_type | solution.py:174
  89.5 18.7 %all_to_all.16 = bf16[4,1024,128]{2,1,0:T(8,128)(2,1)S(1)} all-to-all(bf16[4,1024,128]{2,1,0:T(8,128)(2,1)S(1)} %add_convert_fusion), channel_id=1, replica_groups=mesh['ep'=64,'x'=4,'core'=2] {'x'}, dimensions={0} | all-to-all | bytes 2097152 | tf_op jit(solution)/shard_map/all_to_all | solution.py:175
  108.2 0.1 convert_element_type.24
  108.4 0.8 fusion.3
  109.2 7.1 %all-to-all-start.2 = ((bf16[64,16,128]{2,1,0:T(8,128)(2,1)}), bf16[64,16,128]{2,1,0:T(8,128)(2,1)S(1)}, u32[]{:S(2)}, u32[]{:S(2)}) async-start(bf16[64,16,128]{2,1,0:T(8,128)(2,1)} %bitcast.4), calls=%async_computation.2 | async-start | bytes 524288 | tf_op jit(solution)/shard_map/all_to_all | solution.py:179
  116.4 0.0 copy-start.5
  116.4 2.3 %fusion = bf16[1,1024,512]{2,1,0:T(8,128)(2,1)} fusion(bf16[1024,1024]{1,0:T(8,128)(2,1)S(1)} %copy-done.10, bf16[1024,512]{1,0:T(8,128)(2,1)S(1)} %copy-done.11), kind=kOutput, calls=%fused_computation.3 | convolution fusion | flops 1074266112 | bytes 4194304 | tf_op jit(solution)/shard_map/dot_general | solution.py:181
  118.6 2.2 %fusion.1 = bf16[1,512,1024]{2,1,0:T(8,128)(2,1)} fusion(bf16[1024,512]{1,0:T(8,128)(2,1)S(1)} %copy-done.5, bf16[1024,1024]{1,0:T(8,128)(2,1)S(1)} %copy-done.1), kind=kOutput, calls=%fused_computation.4 | convolution fusion | flops 1074266112 | bytes 4194304 | tf_op jit(solution)/shard_map/dot_general | solution.py:180
  120.9 9.2 %all-to-all-done.2.slots_ref = bf16[64,16,128]{2,1,0:T(8,128)(2,1)S(1)} async-done(((bf16[64,16,128]{2,1,0:T(8,128)(2,1)}), bf16[64,16,128]{2,1,0:T(8,128)(2,1)S(1)}, u32[]{:S(2)}, u32[]{:S(2)}) %all-to-all-start.2) | async-done | bytes 262176 | tf_op jit(solution)/shard_map/all_to_all | solution.py:179
  130.1 0.7 copy-done.4
  130.8 2.7 %unfill_slots.1 = bf16[512,128]{1,0:T(8,128)(2,1)} custom-call(s32[1,64]{1,0:T(1,128)} %counts_ref.3, bf16[64,16,128]{2,1,0:T(8,128)(2,1)} %copy-done.4), custom_call_target="tpu_custom_call" | custom-call | tf_op jit(solution)/shard_map/unfill_slots/pallas_call | solution.py:54
  (27 shorter events, 0.1 us)
Async XLA Ops:
  39.4 32.6 %copy-start = (bf16[64,2,16,128]{3,2,1,0:T(8,128)(2,1)}, bf16[64,2,16,128]{3,2,1,0:T(8,128)(2,1)S(1)}, u32[]{:S(2)}) copy-start(bf16[64,2,16,128]{3,2,1,0:T(8,128)(2,1)S(1)} %all_to_all.15.own) | copy-start | bytes 1572868
  39.4 13.6 %collective-permute-start.1 = (bf16[64,2,16,128]{3,2,1,0:T(8,128)(2,1)S(1)}, bf16[64,2,16,128]{3,2,1,0:T(8,128)(2,1)S(1)}, u32[]{:S(2)}, u32[]{:S(2)}) collective-permute-start(bf16[64,2,16,128]{3,2,1,0:T(8,128)(2,1)S(1)} %all_to_all.15.own), channel_id=1, source_target_pairs={{0,6},{2,0},{4,2},{6,4},{1,7},{3,1},{5,3},{7,5},{8,14},{10,8},{12,... | collective-permute-start | bytes 1572872 | tf_op jit(solution)/shard_map/ppermute | solution.py:150
  44.1 14.5 %collective-permute-start = (bf16[64,2,16,128]{3,2,1,0:T(8,128)(2,1)S(1)}, bf16[64,2,16,128]{3,2,1,0:T(8,128)(2,1)S(1)}, u32[]{:S(2)}, u32[]{:S(2)}) collective-permute-start(bf16[64,2,16,128]{3,2,1,0:T(8,128)(2,1)S(1)} %all_to_all.15.own), channel_id=1, source_target_pairs={{0,2},{2,4},{4,6},{6,0},{1,3},{3,5},{5,7},{7,1},{8,10},{10,12},{12... | collective-permute-start | bytes 1572872 | tf_op jit(solution)/shard_map/ppermute | solution.py:146
  46.0 24.8 %collective-permute-start.4 = (bf16[64,2,16,128]{3,2,1,0:T(8,128)(2,1)S(1)}, bf16[64,2,16,128]{3,2,1,0:T(8,128)(2,1)S(1)}, u32[]{:S(2)}, u32[]{:S(2)}) collective-permute-start(bf16[64,2,16,128]{3,2,1,0:T(8,128)(2,1)S(1)} %all_to_all.15.own), channel_id=1, source_target_pairs={{0,1},{1,0},{2,3},{3,2},{4,5},{5,4},{6,7},{7,6},{8,9},{9,8},{10,11... | collective-permute-start | bytes 1572872 | tf_op jit(solution)/shard_map/ppermute | solution.py:154
  53.0 19.1 %copy-start.2 = (bf16[64,2,16,128]{3,2,1,0:T(8,128)(2,1)}, bf16[64,2,16,128]{3,2,1,0:T(8,128)(2,1)S(1)}, u32[]{:S(2)}) copy-start(bf16[64,2,16,128]{3,2,1,0:T(8,128)(2,1)S(1)} %collective-permute-done.1.right) | copy-start | bytes 1572868
  53.0 11.9 %collective-permute-start.3 = (bf16[32,2,16,128]{3,2,1,0:T(8,128)(2,1)S(1)}, bf16[32,2,16,128]{3,2,1,0:T(8,128)(2,1)S(1)}, u32[]{:S(2)}, u32[]{:S(2)}) collective-permute-start(bf16[32,2,16,128]{3,2,1,0:T(8,128)(2,1)S(1)} %slice.25), channel_id=1, source_target_pairs={{0,6},{2,0},{4,2},{6,4},{1,7},{3,1},{5,3},{7,5},{8,14},{10,8},{12,... | collective-permute-start | bytes 786440 | tf_op jit(solution)/shard_map/ppermute | solution.py:150
  58.6 13.4 %copy-start.3 = (bf16[64,2,16,128]{3,2,1,0:T(8,128)(2,1)}, bf16[64,2,16,128]{3,2,1,0:T(8,128)(2,1)S(1)}, u32[]{:S(2)}) copy-start(bf16[64,2,16,128]{3,2,1,0:T(8,128)(2,1)S(1)} %collective-permute-done.left) | copy-start | bytes 1572868
  58.7 9.6 %collective-permute-start.2 = (bf16[32,2,16,128]{3,2,1,0:T(8,128)(2,1)S(1)}, bf16[32,2,16,128]{3,2,1,0:T(8,128)(2,1)}, u32[]{:S(2)}, u32[]{:S(2)}) collective-permute-start(bf16[32,2,16,128]{3,2,1,0:T(8,128)(2,1)S(1)} %slice.24), channel_id=1, source_target_pairs={{0,2},{2,4},{4,6},{6,0},{1,3},{3,5},{5,7},{7,1},{8,10},{10,12},{12... | collective-permute-start | bytes 786440 | tf_op jit(solution)/shard_map/ppermute | solution.py:146
  60.6 11.4 %collective-permute-start.6 = (bf16[64,2,16,128]{3,2,1,0:T(8,128)(2,1)S(1)}, bf16[64,2,16,128]{3,2,1,0:T(8,128)(2,1)S(1)}, u32[]{:S(2)}, u32[]{:S(2)}) collective-permute-start(bf16[64,2,16,128]{3,2,1,0:T(8,128)(2,1)S(1)} %collective-permute-done.1.right), channel_id=1, source_target_pairs={{0,1},{1,0},{2,3},{3,2},{4,5},{5,4},{6,7},{7,6},{8,9},{9,8},{10,11... | collective-permute-start | bytes 1572872 | tf_op jit(solution)/shard_map/ppermute | solution.py:154
  62.5 9.5 %collective-permute-start.5 = (bf16[64,2,16,128]{3,2,1,0:T(8,128)(2,1)S(1)}, bf16[64,2,16,128]{3,2,1,0:T(8,128)(2,1)S(1)}, u32[]{:S(2)}, u32[]{:S(2)}) collective-permute-start(bf16[64,2,16,128]{3,2,1,0:T(8,128)(2,1)S(1)} %collective-permute-done.left), channel_id=1, source_target_pairs={{0,1},{1,0},{2,3},{3,2},{4,5},{5,4},{6,7},{7,6},{8,9},{9,8},{10,11... | collective-permute-start | bytes 1572872 | tf_op jit(solution)/shard_map/ppermute | solution.py:154
  64.9 7.1 %copy-start.9 = (bf16[32,2,16,128]{3,2,1,0:T(8,128)(2,1)}, bf16[32,2,16,128]{3,2,1,0:T(8,128)(2,1)S(1)}, u32[]{:S(2)}) copy-start(bf16[32,2,16,128]{3,2,1,0:T(8,128)(2,1)S(1)} %collective-permute-done.3.far_hi) | copy-start | bytes 786436
  65.0 5.8 %collective-permute-start.8 = (bf16[32,2,16,128]{3,2,1,0:T(8,128)(2,1)S(1)}, bf16[32,2,16,128]{3,2,1,0:T(8,128)(2,1)}, u32[]{:S(2)}, u32[]{:S(2)}) collective-permute-start(bf16[32,2,16,128]{3,2,1,0:T(8,128)(2,1)S(1)} %collective-permute-done.3.far_hi), channel_id=1, source_target_pairs={{0,1},{1,0},{2,3},{3,2},{4,5},{5,4},{6,7},{7,6},{8,9},{9,8},{10,11... | collective-permute-start | bytes 786440 | tf_op jit(solution)/shard_map/ppermute | solution.py:154
  68.2 3.8 %collective-permute-start.7 = (bf16[32,2,16,128]{3,2,1,0:T(8,128)(2,1)}, bf16[32,2,16,128]{3,2,1,0:T(8,128)(2,1)}, u32[]{:S(2)}, u32[]{:S(2)}) collective-permute-start(bf16[32,2,16,128]{3,2,1,0:T(8,128)(2,1)} %collective-permute-done.2.far_lo), channel_id=1, source_target_pairs={{0,1},{1,0},{2,3},{3,2},{4,5},{5,4},{6,7},{7,6},{8,9},{9,8},{10,11... | collective-permute-start | bytes 786440 | tf_op jit(solution)/shard_map/ppermute | solution.py:154
  70.8 1.3 copy-start.6
  72.0 0.8 copy-start.7
  72.0 1.0 copy-start.8
  82.9 4.8 %collective-permute-start.9 = (bf16[4,1024,128]{2,1,0:T(8,128)(2,1)}, bf16[4,1024,128]{2,1,0:T(8,128)(2,1)S(1)}, u32[]{:S(2)}, u32[]{:S(2)}) collective-permute-start(bf16[4,1024,128]{2,1,0:T(8,128)(2,1)} %get-tuple-element.10), channel_id=1, source_target_pairs={{0,1},{1,0},{2,3},{3,2},{4,5},{5,4},{6,7},{7,6},{8,9},{9,8},{10,11... | collective-permute-start | bytes 3145736 | tf_op jit(solution)/shard_map/ppermute | solution.py:154
  108.2 8.1 %copy-start.11 = (bf16[1024,512]{1,0:T(8,128)(2,1)S(1)}, bf16[1024,512]{1,0:T(8,128)(2,1)}, u32[]{:S(2)}) copy-start(bf16[1024,512]{1,0:T(8,128)(2,1)} %get-tuple-element.12) | copy-start | bytes 3145732
  108.4 8.0 %copy-start.10 = (bf16[1024,1024]{1,0:T(8,128)(2,1)S(1)}, bf16[1024,1024]{1,0:T(8,128)(2,1)}, u32[]{:S(2)}) copy-start(bf16[1024,1024]{1,0:T(8,128)(2,1)} %get-tuple-element.11) | copy-start | bytes 6291460
  109.2 20.9 %all-to-all-start.2 = ((bf16[64,16,128]{2,1,0:T(8,128)(2,1)}), bf16[64,16,128]{2,1,0:T(8,128)(2,1)S(1)}, u32[]{:S(2)}, u32[]{:S(2)}) async-start(bf16[64,16,128]{2,1,0:T(8,128)(2,1)} %bitcast.4), calls=%async_computation.2 | async-start | bytes 524288 | tf_op jit(solution)/shard_map/all_to_all | solution.py:179
  116.3 2.3 %copy-start.1 = (bf16[1024,1024]{1,0:T(8,128)(2,1)S(1)}, bf16[1024,1024]{1,0:T(8,128)(2,1)}, u32[]{:S(2)}) copy-start(bf16[1024,1024]{1,0:T(8,128)(2,1)} %get-tuple-element.14) | copy-start | bytes 6291460
  116.4 2.3 %copy-start.5 = (bf16[1024,512]{1,0:T(8,128)(2,1)S(1)}, bf16[1024,512]{1,0:T(8,128)(2,1)}, u32[]{:S(2)}) copy-start(bf16[1024,512]{1,0:T(8,128)(2,1)} %get-tuple-element.13) | copy-start | bytes 3145732
  130.0 0.7 copy-start.4
